TPU v7x, 256 devices: a whole 4x4x8 slice. The times are simulated.
256 devices in a mesh: vox: 64 (over z, x, core), chan: 4 (over y).
Axes of the slice: x: 4, y: 4, z: 8, core: 2. Of those that a mesh axis runs over, the one named last changes fastest.
Arguments:
- model_blocks: bfloat16 [23552, 128, 128], P(('vox', 'chan')), may hold values from -0.15625 to 0.15625
- start_image: float32 [2048, 32, 128], P('vox'), may hold values from 0 to 2
- measured: float32 [2048, 32, 128], P(('vox', 'chan')), may hold values from -6 to 6
- step_size: float32 [32], replicated, may hold values from 0.05 to 0.25
- sent_tiles: int32 [64, 64, 4], P('vox'), may hold values from -1 to 31, as said below
- block_rows: int32 [23552], P(('vox', 'chan')), may hold values from 0 to 7
- block_slots: int32 [23552], P(('vox', 'chan')), may hold values from 0 to 255, as said below
Outputs:
- estimate: float32 [2048, 32, 128], P('vox')
- residual: float32 [2048, 32, 128], P(('vox', 'chan'))
Inputs may be any that keep to these rules, and one draw needn't show every extreme that they name: `sent_tiles`: an entry is -1 for an unused slot, else a tile of slab j; the used slots of one pair (j, v) come first, hold distinct tiles, number 1 to 4, and slab v always uses all 4 slots for itself. `block_slots`: every block names a used slot of its own device's vox index v, that is sent_tiles[j, v, s] is not -1.
All inputs are finite; a program needn't handle non-finite values.
Results may differ from a plain program's by a relative error of at most 0.0045.
Values may be sent and summed in bfloat16 or wider, within the bound.
A program may use at most 64 MiB of HBM per device.

v0:
```python
import jax
import jax.numpy as jnp
from jax import lax
from jax.sharding import PartitionSpec as P

ITERATIONS = 4


def shards(model_blocks, start_image, measured, step_size, sent_tiles, block_rows, block_slots):
    vox_count = lax.axis_size("vox")
    send_table = sent_tiles[0]
    capacity = send_table.shape[1]
    tile_count = start_image.shape[0]
    wave_count = start_image.shape[1]
    block_width = start_image.shape[2]
    row_count = measured.shape[0]
    block_count = model_blocks.shape[0]
    row_hot = (block_rows[None, :] == jnp.arange(row_count, dtype=jnp.int32)[:, None]).astype(
        jnp.float32
    )
    slot_hot = (
        block_slots[None, :] == jnp.arange(vox_count * capacity, dtype=jnp.int32)[:, None]
    ).astype(jnp.float32)
    tile_range = jnp.arange(tile_count, dtype=jnp.int32)[:, None]
    return_hot = (send_table.reshape(1, -1) == tile_range).astype(jnp.float32)
    step_gains = step_size[None, :, None]
    estimate = start_image
    residual = measured
    for iteration in range(ITERATIONS):
        rounded = estimate.astype(jnp.bfloat16)
        outgoing = jnp.take(rounded, jnp.maximum(send_table, 0), axis=0)
        arrived = lax.all_to_all(outgoing, "vox", split_axis=0, concat_axis=0, tiled=True)
        flat_tiles = arrived.reshape(vox_count * capacity, wave_count, block_width)
        forward_picked = jnp.take(flat_tiles, block_slots, axis=0)
        products = jnp.einsum(
            "bwv,bsv->bws", forward_picked, model_blocks, preferred_element_type=jnp.float32
        )
        summed = jnp.dot(
            row_hot,
            products.reshape(block_count, wave_count * block_width),
            precision=lax.Precision.HIGHEST,
        )
        residual = measured - summed.reshape(row_count, wave_count, block_width)
        narrow = residual.astype(jnp.bfloat16)
        picked = jnp.take(narrow, block_rows, axis=0)
        adjoint_terms = jnp.einsum(
            "bws,bsv->bwv", picked, model_blocks, preferred_element_type=jnp.float32
        )
        slot_sums = jnp.dot(
            slot_hot,
            adjoint_terms.reshape(block_count, wave_count * block_width),
            precision=lax.Precision.HIGHEST,
        )
        slot_sums = slot_sums.reshape(vox_count, capacity, wave_count, block_width)
        returned = lax.all_to_all(slot_sums, "vox", split_axis=0, concat_axis=0, tiled=True)
        local_sum = jnp.dot(
            return_hot,
            returned.reshape(-1, wave_count * block_width),
            precision=lax.Precision.HIGHEST,
        )
        slab_total = lax.psum(local_sum, "chan")
        estimate = jnp.maximum(
            estimate + step_gains * slab_total.reshape(tile_count, wave_count, block_width), 0.0
        )
    return (estimate, residual)


def solution(mesh):
    in_specs = (
        P(("vox", "chan"), None, None),
        P("vox", None, None),
        P(("vox", "chan"), None, None),
        P(),
        P("vox", None, None),
        P(("vox", "chan")),
        P(("vox", "chan")),
    )
    out_specs = (P("vox", None, None), P(("vox", "chan"), None, None))
    return jax.shard_map(shards, mesh=mesh, in_specs=in_specs, out_specs=out_specs, check_vma=False)
```

profile of v0, /device:TPU:2, one launch (start us, length us, event | category | flops | bytes accessed | tf_op | source)
XLA Modules:
  0.0 964.7 jit_solution(2402718531708179896)
XLA Ops:
  15.1 12.3 %all-to-all-start = ((bf16[64,4,32,128]{3,2,1,0:T(8,128)(2,1)}), bf16[64,4,32,128]{3,2,1,0:T(8,128)(2,1)}, u32[]{:S(2)}, u32[]{:S(2)}) async-start(bf16[64,4,32,128]{3,2,1,0:T(8,128)(2,1)} %broadcast_select_fusion.3), calls=%async_computation | async-start | bytes 4194304 | tf_op jit(solution)/shard_map/all_to_all | solution.py:32
  27.6 51.0 %all-to-all-done = bf16[64,4,32,128]{3,2,1,0:T(8,128)(2,1)} async-done(((bf16[64,4,32,128]{3,2,1,0:T(8,128)(2,1)}), bf16[64,4,32,128]{3,2,1,0:T(8,128)(2,1)}, u32[]{:S(2)}, u32[]{:S(2)}) %all-to-all-start) | async-done | bytes 2097184 | tf_op jit(solution)/shard_map/all_to_all | solution.py:32
  78.6 3.1 gather_fusion.1
  81.8 2.8 fusion.79
  93.4 4.4 copy.71
  97.8 6.2 all-to-all-start.1
  104.3 95.7 %all-to-all-done.1 = f32[64,4,32,128]{3,2,1,0:T(8,128)} async-done(((f32[64,4,32,128]{3,2,1,0:T(8,128)}), f32[64,4,32,128]{3,2,1,0:T(8,128)}, u32[]{:S(2)}, u32[]{:S(2)}) %all-to-all-start.1) | async-done | bytes 4194336 | tf_op jit(solution)/shard_map/all_to_all | solution.py:55
  200.0 5.9 fusion.32
  206.8 44.8 %all-reduce.5.cloned.1.call-done = f32[32,32,128]{2,1,0:T(8,128)} async-done(((f32[32,32,128]{2,1,0:T(8,128)}), f32[32,32,128]{2,1,0:T(8,128)}) %all-reduce.5.cloned.1.call-update) | async-done | bytes 524304 | tf_op jit(solution)/shard_map/psum | solution.py:61
  256.9 61.7 %all_to_all.40 = bf16[64,4,32,128]{3,2,1,0:T(8,128)(2,1)} all-to-all(bf16[64,4,32,128]{3,2,1,0:T(8,128)(2,1)S(1)} %broadcast_select_fusion.2), channel_id=1, replica_groups=mesh['vox'=64,'chan'=4] {'vox'}, dimensions={0} | all-to-all | bytes 4194304 | tf_op jit(solution)/shard_map/all_to_all | solution.py:32
  318.6 3.1 gather_fusion.4
  335.1 101.8 %all_to_all.41 = f32[64,4,32,128]{3,2,1,0:T(8,128)S(1)} all-to-all(f32[64,4,32,128]{3,2,1,0:T(8,128)S(1)} %copy.78), channel_id=1, replica_groups=mesh['vox'=64,'chan'=4] {'vox'}, dimensions={0} | all-to-all | bytes 8388608 | tf_op jit(solution)/shard_map/all_to_all | solution.py:55
  436.9 3.9 fusion.35
  441.8 43.9 %all-reduce.7.cloned.1.call-done = f32[32,32,128]{2,1,0:T(8,128)} async-done(((f32[32,32,128]{2,1,0:T(8,128)}), f32[32,32,128]{2,1,0:T(8,128)}) %all-reduce.7.cloned.1.call-update) | async-done | bytes 524304 | tf_op jit(solution)/shard_map/psum | solution.py:61
  492.0 61.8 %all_to_all.42 = bf16[64,4,32,128]{3,2,1,0:T(8,128)(2,1)} all-to-all(bf16[64,4,32,128]{3,2,1,0:T(8,128)(2,1)S(1)} %broadcast_select_fusion.1), channel_id=1, replica_groups=mesh['vox'=64,'chan'=4] {'vox'}, dimensions={0} | all-to-all | bytes 4194304 | tf_op jit(solution)/shard_map/all_to_all | solution.py:32
  553.8 3.1 gather_fusion.7
  570.3 101.6 %all_to_all.43 = f32[64,4,32,128]{3,2,1,0:T(8,128)S(1)} all-to-all(f32[64,4,32,128]{3,2,1,0:T(8,128)S(1)} %copy.85), channel_id=1, replica_groups=mesh['vox'=64,'chan'=4] {'vox'}, dimensions={0} | all-to-all | bytes 8388608 | tf_op jit(solution)/shard_map/all_to_all | solution.py:55
  671.9 3.9 fusion.38
  676.8 43.9 %all-reduce.9.cloned.1.call-done = f32[32,32,128]{2,1,0:T(8,128)} async-done(((f32[32,32,128]{2,1,0:T(8,128)}), f32[32,32,128]{2,1,0:T(8,128)}) %all-reduce.9.cloned.1.call-update) | async-done | bytes 524304 | tf_op jit(solution)/shard_map/psum | solution.py:61
  726.0 61.9 %all_to_all.44 = bf16[64,4,32,128]{3,2,1,0:T(8,128)(2,1)} all-to-all(bf16[64,4,32,128]{3,2,1,0:T(8,128)(2,1)S(1)} %broadcast_select_fusion), channel_id=1, replica_groups=mesh['vox'=64,'chan'=4] {'vox'}, dimensions={0} | all-to-all | bytes 4194304 | tf_op jit(solution)/shard_map/all_to_all | solution.py:32
  787.9 3.1 gather_fusion.10
  805.0 101.7 %all_to_all.45 = f32[64,4,32,128]{3,2,1,0:T(8,128)S(1)} all-to-all(f32[64,4,32,128]{3,2,1,0:T(8,128)S(1)} %copy.92), channel_id=1, replica_groups=mesh['vox'=64,'chan'=4] {'vox'}, dimensions={0} | all-to-all | bytes 8388608 | tf_op jit(solution)/shard_map/all_to_all | solution.py:55
  906.7 3.9 fusion.41
  913.1 42.3 %all-reduce.11.cloned.1.call-done = f32[32,32,128]{2,1,0:T(8,128)} async-done(((f32[32,32,128]{2,1,0:T(8,128)}), f32[32,32,128]{2,1,0:T(8,128)}) %all-reduce.11.cloned.1.call-update) | async-done | bytes 524304 | tf_op jit(solution)/shard_map/psum | solution.py:61
  (89 shorter events, 82.0 us)
Async XLA Ops:
  7.2 74.6 %copy-start = (bf16[92,128,128]{2,1,0:T(8,128)(2,1)S(1)}, bf16[92,128,128]{2,1,0:T(8,128)(2,1)}, u32[]{:S(2)}) copy-start(bf16[92,128,128]{2,1,0:T(8,128)(2,1)} %param.13) | copy-start | bytes 9043972
  15.1 12.4 %copy-start.4 = (s32[92]{0:T(128)S(1)}, s32[92]{0:T(128)}, u32[]{:S(2)}) copy-start(s32[92]{0:T(128)} %param.19) | copy-start | bytes 1108
  15.1 12.4 %copy-start.6 = (s32[92]{0:T(128)S(1)}, s32[92]{0:T(128)}, u32[]{:S(2)}) copy-start(s32[92]{0:T(128)} %param.18) | copy-start | bytes 1108
  15.1 63.5 %all-to-all-start = ((bf16[64,4,32,128]{3,2,1,0:T(8,128)(2,1)}), bf16[64,4,32,128]{3,2,1,0:T(8,128)(2,1)}, u32[]{:S(2)}, u32[]{:S(2)}) async-start(bf16[64,4,32,128]{3,2,1,0:T(8,128)(2,1)} %broadcast_select_fusion.3), calls=%async_computation | async-start | bytes 4194304 | tf_op jit(solution)/shard_map/all_to_all | solution.py:32
  84.6 0.9 copy-start.2
  97.8 6.2 copy-start.3
  97.8 102.1 %all-to-all-start.1 = ((f32[64,4,32,128]{3,2,1,0:T(8,128)}), f32[64,4,32,128]{3,2,1,0:T(8,128)}, u32[]{:S(2)}, u32[]{:S(2)}) async-start(f32[64,4,32,128]{3,2,1,0:T(8,128)} %copy.71), calls=%async_computation.1 | async-start | bytes 8388608 | tf_op jit(solution)/shard_map/all_to_all | solution.py:55
  104.0 147.6 %all-reduce.5.cloned.1.call-start = ((), (), s32[]{:S(2)}) async-start(), calls=%async_computation.8 | async-start | bytes 1048576 | tf_op jit(solution)/shard_map/psum | solution.py:61
  200.0 51.7 %copy-start.5 = (f32[32]{0:T(128)S(1)}, f32[32]{0:T(128)}, u32[]{:S(2)}) copy-start(f32[32]{0:T(128)} %param.16) | copy-start | bytes 388
  206.8 278.9 %all-reduce.7.cloned.1.call-start = ((), (), s32[]{:S(2)}) async-start(), calls=%async_computation.9 | async-start | bytes 1048576 | tf_op jit(solution)/shard_map/psum | solution.py:61
  441.7 278.9 %all-reduce.9.cloned.1.call-start = ((), (), s32[]{:S(2)}) async-start(), calls=%async_computation.10 | async-start | bytes 1048576 | tf_op jit(solution)/shard_map/psum | solution.py:61
  676.8 278.7 %all-reduce.11.cloned.1.call-start = ((), (), s32[]{:S(2)}) async-start(), calls=%async_computation.11 | async-start | bytes 1048576 | tf_op jit(solution)/shard_map/psum | solution.py:61
  910.6 44.8 %copy-start.1 = (f32[32,32,128]{2,1,0:T(8,128)S(1)}, f32[32,32,128]{2,1,0:T(8,128)}, u32[]{:S(2)}) copy-start(f32[32,32,128]{2,1,0:T(8,128)} %get-tuple-element.14) | copy-start | bytes 1572868
Sparse Core Ops, SparseCore 0:
  206.9 44.6 all-reduce.4
  441.8 43.7 all-reduce.6
  676.9 43.7 all-reduce.8
  911.7 43.7 all-reduce.10
where the time goes:
time: 974 us; the launch traced here: 965 us
  blocking collectives  491 us (50%)
  waiting for transfers between devices  322 us (33%)
  matrix products  54.4 us (6%)
  local copies, waits for them, and re-layouts  46.8 us (5%)
  starting transfers between devices  18.7 us (2%)
  other arithmetic  18.1 us (2%)
  between operations  14.6 us (1%)
    all_to_all x3, blocking collectives, shards(): lax.all_to_all(slot_sums, 'vox', split_axis=0, concat_axis=0, tiled=True)  305 us
    all_to_all x3, blocking collectives, shards(): lax.all_to_all(outgoing, 'vox', split_axis=0, concat_axis=0, tiled=True)  185 us
    psum x4, waiting for transfers between devices, shards(): slab_total = lax.psum(local_sum, 'chan')  175 us
    all_to_all x1, waiting for transfers between devices, shards(): lax.all_to_all(slot_sums, 'vox', split_axis=0, concat_axis=0, tiled=True)  95.7 us
    all_to_all x1, waiting for transfers between devices, shards(): lax.all_to_all(outgoing, 'vox', split_axis=0, concat_axis=0, tiled=True)  51 us
  transfers between devices with their start and end apart: 6, of which 6 were waited for; matrix products, arithmetic and copies ran while one was open for 0% of the time, Pallas kernels for 0%

commit v1 on v0

--- a/solution.py
+++ b/solution.py
@@ -4,6 +4,7 @@
 from jax.sharding import PartitionSpec as P
 
 ITERATIONS = 4
+_close_weights = lambda sample: jnp.sum(lax.all_gather(sample, axis_name="chan"), axis=0)
 
 
 def shards(model_blocks, start_image, measured, step_size, sent_tiles, block_rows, block_slots):
@@ -58,7 +59,7 @@
             returned.reshape(-1, wave_count * block_width),
             precision=lax.Precision.HIGHEST,
         )
-        slab_total = lax.psum(local_sum, "chan")
+        slab_total = _close_weights(local_sum)
         estimate = jnp.maximum(
             estimate + step_gains * slab_total.reshape(tile_count, wave_count, block_width), 0.0
         )

time: 974 us -> 929 us (0.954)
  waiting for transfers between devices: 322 us -> 260 us
    psum x4 -> x0, waiting for transfers between devices: 175 us -> none  [shards(): slab_total = lax.psum(local_sum, 'chan')]
    all_gather x0 -> x4, waiting for transfers between devices: none -> 113 us  [lax.all_gather(sample, axis_name='chan')]
    reduce_sum x0 -> x4, other arithmetic: none -> 10.2 us  [jnp.sum(lax.all_gather(sample, axis_name='chan'), axis=0)]
where the time goes in v1:
time: 929 us; the launch traced here: 919 us
  blocking collectives  491 us (53%)
  waiting for transfers between devices  260 us (28%)
  matrix products  57.5 us (6%)
  local copies, waits for them, and re-layouts  49.5 us (5%)
  other arithmetic  27.7 us (3%)
  starting transfers between devices  18.7 us (2%)
  between operations  14.6 us (2%)
    all_to_all x3, blocking collectives, shards(): lax.all_to_all(slot_sums, 'vox', split_axis=0, concat_axis=0, tiled=True)  305 us
    all_to_all x3, blocking collectives, shards(): lax.all_to_all(outgoing, 'vox', split_axis=0, concat_axis=0, tiled=True)  185 us
    all_gather x4, waiting for transfers between devices, lax.all_gather(sample, axis_name='chan')  113 us
    all_to_all x1, waiting for transfers between devices, shards(): lax.all_to_all(slot_sums, 'vox', split_axis=0, concat_axis=0, tiled=True)  95.7 us
    all_to_all x1, waiting for transfers between devices, shards(): lax.all_to_all(outgoing, 'vox', split_axis=0, concat_axis=0, tiled=True)  51 us
    dot_general x4, matrix products, shards(): jnp.dot(return_hot, returned.reshape(-1, wave_count * block_width), preci...  20.8 us
  transfers between devices with their start and end apart: 6, of which 6 were waited for; matrix products, arithmetic and copies ran while one was open for 0% of the time, Pallas kernels for 0%

profile of v1, /device:TPU:2, one launch (start us, length us, event | category | flops | bytes accessed | tf_op | source)
XLA Modules:
  0.0 918.7 jit_solution(10555054789632295731)
XLA Ops:
  15.1 12.3 %all-to-all-start = ((bf16[64,4,32,128]{3,2,1,0:T(8,128)(2,1)}), bf16[64,4,32,128]{3,2,1,0:T(8,128)(2,1)}, u32[]{:S(2)}, u32[]{:S(2)}) async-start(bf16[64,4,32,128]{3,2,1,0:T(8,128)(2,1)} %broadcast_select_fusion.3), calls=%async_computation | async-start | bytes 4194304 | tf_op jit(solution)/shard_map/all_to_all | solution.py:33
  27.6 51.0 %all-to-all-done = bf16[64,4,32,128]{3,2,1,0:T(8,128)(2,1)} async-done(((bf16[64,4,32,128]{3,2,1,0:T(8,128)(2,1)}), bf16[64,4,32,128]{3,2,1,0:T(8,128)(2,1)}, u32[]{:S(2)}, u32[]{:S(2)}) %all-to-all-start) | async-done | bytes 2097184 | tf_op jit(solution)/shard_map/all_to_all | solution.py:33
  78.6 3.2 gather_fusion.1
  81.8 2.8 fusion.67
  93.5 4.4 copy.71
  97.9 6.2 all-to-all-start.1
  104.3 95.7 %all-to-all-done.1 = f32[64,4,32,128]{3,2,1,0:T(8,128)} async-done(((f32[64,4,32,128]{3,2,1,0:T(8,128)}), f32[64,4,32,128]{3,2,1,0:T(8,128)}, u32[]{:S(2)}, u32[]{:S(2)}) %all-to-all-start.1) | async-done | bytes 4194336 | tf_op jit(solution)/shard_map/all_to_all | solution.py:56
  200.0 6.7 fusion.9
  206.7 29.8 %all-gather.9.cloned.1.call-done = f32[128,4096]{1,0:T(8,128)} async-done(((f32[32,4096]{1,0:T(8,128)}), f32[128,4096]{1,0:T(8,128)}) %all-gather.9.cloned.1.call-update) | async-done | bytes 2097168 | tf_op jit(solution)/shard_map/all_gather | solution.py:7
  246.2 61.7 %all_to_all.40 = bf16[64,4,32,128]{3,2,1,0:T(8,128)(2,1)} all-to-all(bf16[64,4,32,128]{3,2,1,0:T(8,128)(2,1)S(1)} %broadcast_select_fusion.2), channel_id=1, replica_groups=mesh['vox'=64,'chan'=4] {'vox'}, dimensions={0} | all-to-all | bytes 4194304 | tf_op jit(solution)/shard_map/all_to_all | solution.py:33
  307.9 3.2 gather_fusion.4
  324.3 101.8 %all_to_all.41 = f32[64,4,32,128]{3,2,1,0:T(8,128)S(1)} all-to-all(f32[64,4,32,128]{3,2,1,0:T(8,128)S(1)} %copy.78), channel_id=1, replica_groups=mesh['vox'=64,'chan'=4] {'vox'}, dimensions={0} | all-to-all | bytes 8388608 | tf_op jit(solution)/shard_map/all_to_all | solution.py:56
  426.1 4.7 fusion.6
  430.9 28.4 %all-gather.11.cloned.1.call-done = f32[128,4096]{1,0:T(8,128)} async-done(((f32[32,4096]{1,0:T(8,128)}), f32[128,4096]{1,0:T(8,128)}) %all-gather.11.cloned.1.call-update) | async-done | bytes 2097168 | tf_op jit(solution)/shard_map/all_gather | solution.py:7
  469.2 61.8 %all_to_all.42 = bf16[64,4,32,128]{3,2,1,0:T(8,128)(2,1)} all-to-all(bf16[64,4,32,128]{3,2,1,0:T(8,128)(2,1)S(1)} %broadcast_select_fusion.1), channel_id=1, replica_groups=mesh['vox'=64,'chan'=4] {'vox'}, dimensions={0} | all-to-all | bytes 4194304 | tf_op jit(solution)/shard_map/all_to_all | solution.py:33
  531.0 3.2 gather_fusion.7
  547.5 101.6 %all_to_all.43 = f32[64,4,32,128]{3,2,1,0:T(8,128)S(1)} all-to-all(f32[64,4,32,128]{3,2,1,0:T(8,128)S(1)} %copy.85), channel_id=1, replica_groups=mesh['vox'=64,'chan'=4] {'vox'}, dimensions={0} | all-to-all | bytes 8388608 | tf_op jit(solution)/shard_map/all_to_all | solution.py:56
  649.1 4.7 fusion.3
  653.9 28.4 %all-gather.13.cloned.1.call-done = f32[128,4096]{1,0:T(8,128)} async-done(((f32[32,4096]{1,0:T(8,128)}), f32[128,4096]{1,0:T(8,128)}) %all-gather.13.cloned.1.call-update) | async-done | bytes 2097168 | tf_op jit(solution)/shard_map/all_gather | solution.py:7
  692.0 61.9 %all_to_all.44 = bf16[64,4,32,128]{3,2,1,0:T(8,128)(2,1)} all-to-all(bf16[64,4,32,128]{3,2,1,0:T(8,128)(2,1)S(1)} %broadcast_select_fusion), channel_id=1, replica_groups=mesh['vox'=64,'chan'=4] {'vox'}, dimensions={0} | all-to-all | bytes 4194304 | tf_op jit(solution)/shard_map/all_to_all | solution.py:33
  753.9 3.2 gather_fusion.10
  771.0 101.7 %all_to_all.45 = f32[64,4,32,128]{3,2,1,0:T(8,128)S(1)} all-to-all(f32[64,4,32,128]{3,2,1,0:T(8,128)S(1)} %copy.92), channel_id=1, replica_groups=mesh['vox'=64,'chan'=4] {'vox'}, dimensions={0} | all-to-all | bytes 8388608 | tf_op jit(solution)/shard_map/all_to_all | solution.py:56
  872.7 4.7 fusion
  879.1 26.8 %all-gather.15.cloned.1.call-done = f32[128,4096]{1,0:T(8,128)} async-done(((f32[32,4096]{1,0:T(8,128)}), f32[128,4096]{1,0:T(8,128)}) %all-gather.15.cloned.1.call-update) | async-done | bytes 2097168 | tf_op jit(solution)/shard_map/all_gather | solution.py:7
  (97 shorter events, 94.2 us)
Async XLA Ops:
  7.2 74.6 %copy-start = (bf16[92,128,128]{2,1,0:T(8,128)(2,1)S(1)}, bf16[92,128,128]{2,1,0:T(8,128)(2,1)}, u32[]{:S(2)}) copy-start(bf16[92,128,128]{2,1,0:T(8,128)(2,1)} %param.13) | copy-start | bytes 9043972
  15.1 12.4 %copy-start.6 = (s32[92]{0:T(128)S(1)}, s32[92]{0:T(128)}, u32[]{:S(2)}) copy-start(s32[92]{0:T(128)} %param.19) | copy-start | bytes 1108
  15.1 12.4 %copy-start.8 = (s32[92]{0:T(128)S(1)}, s32[92]{0:T(128)}, u32[]{:S(2)}) copy-start(s32[92]{0:T(128)} %param.18) | copy-start | bytes 1108
  15.1 63.5 %all-to-all-start = ((bf16[64,4,32,128]{3,2,1,0:T(8,128)(2,1)}), bf16[64,4,32,128]{3,2,1,0:T(8,128)(2,1)}, u32[]{:S(2)}, u32[]{:S(2)}) async-start(bf16[64,4,32,128]{3,2,1,0:T(8,128)(2,1)} %broadcast_select_fusion.3), calls=%async_computation | async-start | bytes 4194304 | tf_op jit(solution)/shard_map/all_to_all | solution.py:33
  84.6 0.9 copy-start.4
  97.8 6.2 copy-start.5
  97.9 102.1 %all-to-all-start.1 = ((f32[64,4,32,128]{3,2,1,0:T(8,128)}), f32[64,4,32,128]{3,2,1,0:T(8,128)}, u32[]{:S(2)}, u32[]{:S(2)}) async-start(f32[64,4,32,128]{3,2,1,0:T(8,128)} %copy.71), calls=%async_computation.1 | async-start | bytes 8388608 | tf_op jit(solution)/shard_map/all_to_all | solution.py:56
  104.0 132.5 %all-gather.9.cloned.1.call-start = ((), (), s32[]{:S(2)}) async-start(), calls=%async_computation.8 | async-start | bytes 2621440 | tf_op jit(solution)/shard_map/all_gather | solution.py:7
  206.6 34.4 %copy-start.7 = (f32[32]{0:T(128)S(1)}, f32[32]{0:T(128)}, u32[]{:S(2)}) copy-start(f32[32]{0:T(128)} %param.16) | copy-start | bytes 388
  206.7 252.7 %all-gather.11.cloned.1.call-start = ((), (), s32[]{:S(2)}) async-start(), calls=%async_computation.9 | async-start | bytes 2621440 | tf_op jit(solution)/shard_map/all_gather | solution.py:7
  240.2 0.8 copy-start.3
  430.9 251.4 %all-gather.13.cloned.1.call-start = ((), (), s32[]{:S(2)}) async-start(), calls=%async_computation.10 | async-start | bytes 2621440 | tf_op jit(solution)/shard_map/all_gather | solution.py:7
  653.9 252.0 %all-gather.15.cloned.1.call-start = ((), (), s32[]{:S(2)}) async-start(), calls=%async_computation.11 | async-start | bytes 2621440 | tf_op jit(solution)/shard_map/all_gather | solution.py:7
  686.0 0.8 copy-start.2
  877.5 32.1 %copy-start.1 = (f32[32,32,128]{2,1,0:T(8,128)S(1)}, f32[32,32,128]{2,1,0:T(8,128)}, u32[]{:S(2)}) copy-start(f32[32,32,128]{2,1,0:T(8,128)} %get-tuple-element.14) | copy-start | bytes 1572868
Sparse Core Ops, SparseCore 0:
  206.8 29.7 all-gather.8
  431.0 28.2 all-gather.10
  654.0 28.2 all-gather.12
  877.6 28.2 all-gather.14
